TPU v7x, 512 devices: a whole 4x4x16 slice. The times are simulated.
512 devices in a mesh: col: 16 (over z_lo, core), row: 32 (over z_hi, x, y).
Axes of the slice: x: 4, y: 4, z: 16 (z_hi: 2, z_lo: 8; z = z_hi * 8 + z_lo), core: 2. Of those that a mesh axis runs over, the one named last changes fastest.
Arguments:
- tokens: bfloat16 [2048, 8192], P('col', 'row'), may hold values from -6 to 6
- gate_weight: bfloat16 [8192, 14336], P('col', 'row'), may hold values from -0.0625 to 0.0625
- up_weight: bfloat16 [8192, 14336], P('col', 'row'), may hold values from -0.0625 to 0.0625
Outputs:
- hidden: bfloat16 [2048, 14336], P('col', 'row')
All inputs are finite; a program needn't handle non-finite values.
Results may differ from a plain program's by a relative error of at most 0.0012.
Values may be sent and summed in bfloat16 or wider, within the bound.
No kernel may reach another device: no remote copies, remote signals or barrier semaphores. Data moves between devices by JAX's collectives and lax.ppermute only.
A program may use at most 64 MiB of HBM per device.

v0:
```python
import jax
import jax.numpy as jnp
from jax import lax
from jax.sharding import PartitionSpec as P


def add_block(whole, pieces):
    gate_part = jnp.dot(whole, pieces[0], preferred_element_type=jnp.float32)
    up_part = jnp.dot(whole, pieces[1], preferred_element_type=jnp.float32)
    return (gate_part, up_part)


def local(tokens, gate_weight, up_weight):
    whole = lax.all_gather(tokens, "row", axis=1, tiled=True)
    gate, up = add_block(
        whole,
        (
            lax.all_gather(gate_weight, "col", axis=0, tiled=True),
            lax.all_gather(up_weight, "col", axis=0, tiled=True),
        ),
    )
    return (jax.nn.silu(gate) * up).astype(jnp.bfloat16)


def solution(mesh):
    in_specs = (P("col", "row"), P("col", "row"), P("col", "row"))
    out_specs = P("col", "row")
    return jax.shard_map(local, mesh=mesh, in_specs=in_specs, out_specs=out_specs, check_vma=False)
```

profile of v0, /device:TPU:4, one launch (start us, length us, event | category | flops | bytes accessed | tf_op | source)
XLA Modules:
  0.0 390.2 jit_solution(5157250987532368884)
XLA Ops:
  6.5 0.0 all-gather.4.cloned.1.call-start
  6.5 0.7 all-gather.4.cloned.1.call-update
  7.3 0.0 all-gather.6.cloned.1.call-start
  7.3 0.7 all-gather.6.cloned.1.call-update
  8.0 0.0 all-gather.8.cloned.1.call-start
  8.1 0.7 all-gather.8.cloned.1.call-update
  8.7 147.2 %all-gather.4.cloned.1.call-done = bf16[128,8192]{1,0:T(8,128)(2,1)} async-done(((bf16[128,256]{1,0:T(8,128)(2,1)}), bf16[128,8192]{1,0:T(8,128)(2,1)}) %all-gather.4.cloned.1.call-update) | async-done | bytes 2097168 | tf_op jit(solution)/shard_map/all_gather | solution.py:14
  155.9 0.0 copy-start
  155.9 109.7 %all-gather.6.cloned.1.call-done = bf16[8192,448]{0,1:T(8,128)(2,1)} async-done(((bf16[512,448]{0,1:T(8,128)(2,1)}), bf16[8192,448]{0,1:T(8,128)(2,1)}) %all-gather.6.cloned.1.call-update) | async-done | bytes 7340048 | tf_op jit(solution)/shard_map/all_gather | solution.py:18
  265.7 5.8 %fusion.1 = f32[128,448]{0,1:T(8,128)S(1)} fusion(bf16[128,8192]{1,0:T(8,128)(2,1)} %all-gather.4.cloned.1.call-done, bf16[8192,448]{0,1:T(8,128)(2,1)} %all-gather.6.cloned.1.call-done), kind=kOutput, calls=%fused_computation.2 | convolution fusion | flops 939524096 | bytes 9666560 | tf_op jit(solution)/shard_map/dot_general | solution.py:8
  271.5 106.4 %all-gather.8.cloned.1.call-done = bf16[8192,448]{0,1:T(8,128)(2,1)} async-done(((bf16[512,448]{0,1:T(8,128)(2,1)}), bf16[8192,448]{0,1:T(8,128)(2,1)}) %all-gather.8.cloned.1.call-update) | async-done | bytes 7340048 | tf_op jit(solution)/shard_map/all_gather | solution.py:19
  377.9 0.0 copy-done
  377.9 5.8 %fusion = bf16[128,448]{0,1:T(8,128)(2,1)} fusion(bf16[128,8192]{1,0:T(8,128)(2,1)S(1)} %copy-done, bf16[8192,448]{0,1:T(8,128)(2,1)} %all-gather.8.cloned.1.call-done, f32[128,448]{0,1:T(8,128)S(1)} %fusion.1), kind=kOutput, calls=%fused_computation.1 | convolution fusion | flops 939868160 | bytes 9781248 | tf_op jit(solution)/shard_map/dot_general | solution.py:9
Async XLA Ops:
  6.5 149.4 %all-gather.4.cloned.1.call-start = ((), (), s32[]{:S(2)}) async-start(), calls=%async_computation | async-start | bytes 2162688 | tf_op jit(solution)/shard_map/all_gather | solution.py:14
  7.3 258.4 %all-gather.6.cloned.1.call-start = ((), (), s32[]{:S(2)}) async-start(), calls=%async_computation.1 | async-start | bytes 7798784 | tf_op jit(solution)/shard_map/all_gather | solution.py:18
  8.0 369.9 %all-gather.8.cloned.1.call-start = ((), (), s32[]{:S(2)}) async-start(), calls=%async_computation.2 | async-start | bytes 7798784 | tf_op jit(solution)/shard_map/all_gather | solution.py:19
  155.9 221.9 %copy-start = (bf16[128,8192]{1,0:T(8,128)(2,1)S(1)}, bf16[128,8192]{1,0:T(8,128)(2,1)}, u32[]{:S(2)}) copy-start(bf16[128,8192]{1,0:T(8,128)(2,1)} %all-gather.4.cloned.1.call-done) | copy-start | bytes 6291460
Sparse Core Ops, SparseCore 0:
  11.4 144.4 all-gather.3
  158.0 107.6 all-gather.5
  267.8 110.0 all-gather.7
where the time goes:
time: 390 us
  waiting for transfers between devices  365 us (94%)
  between operations  13.1 us (3%)
  matrix products  11.6 us (3%)
    all_gather x1, waiting for transfers between devices, local(): whole = lax.all_gather(tokens, 'row', axis=1, tiled=True)  147 us
    all_gather x1, waiting for transfers between devices, local(): lax.all_gather(gate_weight, 'col', axis=0, tiled=True)  110 us
    all_gather x1, waiting for transfers between devices, local(): lax.all_gather(up_weight, 'col', axis=0, tiled=True)  106 us
  transfers between devices with their start and end apart: 3, of which 3 were waited for; matrix products, arithmetic and copies ran while one was open for 1% of the time, Pallas kernels for 0%

commit v1 on v0

v1 whole, which is shorter than its diff:
```python
import jax
import jax.numpy as jnp
from jax import lax
from jax.sharding import Mesh, PartitionSpec as P

F32 = jnp.float32
AXES = ("zl", "q", "zh", "x", "y")
SIZES = (8, 2, 2, 4, 4)


def local(tokens, gate_weight, up_weight):
    zl, q = lax.axis_index("zl"), lax.axis_index("q")
    own = (gate_weight.T, up_weight.T)
    other = tuple(lax.ppermute(w, "q", [(0, 1), (1, 0)]) for w in own)

    by_x = lax.all_to_all(tokens.reshape(4, 32, 256), "x", 0, 0, tiled=True)
    by_z = lax.all_to_all(jnp.concatenate([by_x] * 4, 0), ("zh", "zl"), 0, 0, tiled=True)
    mine = lax.dynamic_slice_in_dim(by_z, 8 * (zl // 4), 8, 0)
    whole = lax.all_to_all(jnp.broadcast_to(mine[None], (16, 8, 32, 256)), ("x", "y"), 0, 0, tiled=True)
    rows = whole.reshape(4, 4, 8, 32, 256).transpose(0, 2, 3, 1, 4).reshape(1024, 1024)

    sums = []
    for a, b in zip(own, other):
        w = jnp.where(q == 0, jnp.concatenate([a, b], 1), jnp.concatenate([b, a], 1))
        part = lax.dot_general(rows, w, (((1,), (1,)), ((), ())), preferred_element_type=F32)
        sums.append(part.reshape(4, 8, 32, 448))

    def block(k, at):
        return lax.dynamic_index_in_dim(sums[k], jnp.clip(at, 0, 7), 1, False).reshape(128, 448)

    right = [None, None]
    left = [None, None]
    for s in range(1, 8):
        to_right = [(j, j + 1) for j in range(7) if j <= s - 1]
        to_left = [(j, j - 1) for j in range(1, 8) if j >= 8 - s]
        for k in range(2):
            a, b = block(k, zl + 8 - s), block(k, zl - 8 + s)
            if s > 1:
                r, l = lax.optimization_barrier((right[k], left[k]))
                a, b = a + r, b + l
            right[k] = lax.ppermute(a, "zl", to_right)
            left[k] = lax.ppermute(b, "zl", to_left)
    gate, up = (block(k, zl) + right[k] + left[k] for k in range(2))
    return (jax.nn.silu(gate) * up).astype(jnp.bfloat16)


def solution(mesh):
    fine = Mesh(mesh.devices.reshape(SIZES), AXES)
    spec = P(("zl", "q"), ("zh", "x", "y"))
    return jax.shard_map(local, mesh=fine, in_specs=(spec,) * 3, out_specs=spec, check_vma=False)
```

time: 390 us -> 172 us (0.44)
  the two profiles are of different devices: /device:TPU:4 before, /device:TPU:128 now
where the time goes in v1:
time: 172 us
  starting transfers between devices  85.3 us (50%)
  waiting for transfers between devices  65.9 us (38%)
  blocking collectives  9.92 us (6%)
  local copies, waits for them, and re-layouts  4.18 us (2%)
  matrix products  3.77 us (2%)
  other arithmetic  1.76 us (1%)
    ppermute x14, starting transfers between devices, local(): left[k] = lax.ppermute(b, 'zl', to_left)  43 us
    all_to_all x1, waiting for transfers between devices, local(): lax.all_to_all(jnp.broadcast_to(mine[None], (16, 8, 32, 256)), ('x', 'y')...  20.9 us
    ppermute x14, waiting for transfers between devices, local(): left[k] = lax.ppermute(b, 'zl', to_left)  19.7 us
    ppermute x14, starting transfers between devices, local(): right[k] = lax.ppermute(a, 'zl', to_right)  18.7 us
    all_to_all x1, waiting for transfers between devices, local(): lax.all_to_all(jnp.concatenate([by_x] * 4, 0), ('zh', 'zl'), 0, 0, tiled=...  14.6 us
    all_to_all x1, starting transfers between devices, local(): lax.all_to_all(jnp.concatenate([by_x] * 4, 0), ('zh', 'zl'), 0, 0, tiled=...  13.8 us
    ppermute x14, waiting for transfers between devices, local(): right[k] = lax.ppermute(a, 'zl', to_right)  10.8 us
    all_to_all x1, blocking collectives, local(): by_x = lax.all_to_all(tokens.reshape(4, 32, 256), 'x', 0, 0, tiled=True)  9.92 us
  transfers between devices with their start and end apart: 32, of which 12 were waited for; matrix products, arithmetic and copies ran while one was open for 4% of the time, Pallas kernels for 0%

profile of v1, /device:TPU:128, one launch (start us, length us, event | category | flops | bytes accessed | tf_op | source)
XLA Modules:
  0.0 171.5 jit_solution(6057146664306137146)
XLA Ops:
  0.0 9.9 %all_to_all.15 = bf16[4,32,256]{2,1,0:T(8,128)(2,1)S(1)} all-to-all(bf16[4,32,256]{2,1,0:T(8,128)(2,1)} %bitcast.93), channel_id=1, replica_groups=mesh['zl'=8,'q'=2,'zh'=2,'x'=4,'y'=4] {'x'}, dimensions={0} | all-to-all | bytes 131072 | tf_op jit(solution)/shard_map/all_to_all | solution.py:16
  10.6 13.8 %all-to-all-start.1 = ((bf16[16,32,256]{2,1,0:T(8,128)(2,1)}), bf16[16,32,256]{2,1,0:T(8,128)(2,1)S(1)}, u32[]{:S(2)}, u32[]{:S(2)}) async-start(bf16[16,32,256]{2,1,0:T(8,128)(2,1)} %pad_maximum_fusion), calls=%async_computation.1 | async-start | bytes 524288 | tf_op jit(solution)/shard_map/all_to_all | solution.py:17
  24.5 14.6 %all-to-all-done.1 = bf16[16,32,256]{2,1,0:T(8,128)(2,1)S(1)} async-done(((bf16[16,32,256]{2,1,0:T(8,128)(2,1)}), bf16[16,32,256]{2,1,0:T(8,128)(2,1)S(1)}, u32[]{:S(2)}, u32[]{:S(2)}) %all-to-all-start.1) | async-done | bytes 262176 | tf_op jit(solution)/shard_map/all_to_all | solution.py:17
  40.7 5.5 %all-to-all-start.2 = ((bf16[16,8,32,256]{3,2,1,0:T(8,128)(2,1)}), bf16[16,8,32,256]{3,2,1,0:T(8,128)(2,1)S(1)}, u32[]{:S(2)}, u32[]{:S(2)}) async-start(bf16[16,8,32,256]{3,2,1,0:T(8,128)(2,1)} %broadcast_in_dim.2), calls=%async_computation.2 | async-start | bytes 4194304 | tf_op jit(solution)/shard_map/all_to_all | solution.py:19
  46.2 1.9 %collective-permute-start = (bf16[448,512]{1,0:T(8,128)(2,1)S(1)}, bf16[448,512]{1,0:T(8,128)(2,1)}, u32[]{:S(2)}, u32[]{:S(2)}) collective-permute-start(bf16[448,512]{1,0:T(8,128)(2,1)S(1)} %bitcast.94), channel_id=1, source_target_pairs={{0,32},{32,0},{1,33},{33,1},{2,34},{34,2},{3,35},{35,3},{4,36},{36... | collective-permute-start | bytes 1376264 | tf_op jit(solution)/shard_map/ppermute | solution.py:14
  48.1 2.4 %collective-permute-start.15 = (bf16[448,512]{1,0:T(8,128)(2,1)S(1)}, bf16[448,512]{1,0:T(8,128)(2,1)S(1)}, u32[]{:S(2)}, u32[]{:S(2)}) collective-permute-start(bf16[448,512]{1,0:T(8,128)(2,1)S(1)} %bitcast.96), channel_id=1, source_target_pairs={{0,32},{32,0},{1,33},{33,1},{2,34},{34,2},{3,35},{35,3},{4,36},{36... | collective-permute-start | bytes 1376264 | tf_op jit(solution)/shard_map/ppermute | solution.py:14
  50.6 20.9 %all-to-all-done.2 = bf16[16,8,32,256]{3,2,1,0:T(8,128)(2,1)S(1)} async-done(((bf16[16,8,32,256]{3,2,1,0:T(8,128)(2,1)}), bf16[16,8,32,256]{3,2,1,0:T(8,128)(2,1)S(1)}, u32[]{:S(2)}, u32[]{:S(2)}) %all-to-all-start.2) | async-done | bytes 2097184 | tf_op jit(solution)/shard_map/all_to_all | solution.py:19
  71.8 2.5 %fusion.1 = f32[4,8,32,448]{3,2,1,0:T(8,128)S(1)} fusion(bf16[4,8,32,1024]{3,2,1,0:T(8,128)(2,1)S(1)} %bitcast.87, bf16[448,512]{1,0:T(8,128)(2,1)} %collective-permute-done, bf16[448,512]{1,0:T(8,128)(2,1)S(1)} %bitcast.95, pred[]{:T(512)S(6)} %eq.4), kind=kOutput, calls=%fused_computation.2 | convolution fusion | flops 943652864 | bytes 4849665 | tf_op jit(solution)/shard_map/dot_general | solution.py:25
  87.0 18.1 %collective-permute-done.6 = f32[128,448]{1,0:T(8,128)S(1)} collective-permute-done((f32[128,448]{1,0:T(8,128)S(1)}, f32[128,448]{1,0:T(8,128)S(1)}, u32[]{:S(2)}, u32[]{:S(2)}) %collective-permute-start.6) | collective-permute-done | bytes 229408 | tf_op jit(solution)/shard_map/ppermute | solution.py:42
  105.1 5.7 %collective-permute-start.8 = (f32[128,448]{1,0:T(8,128)S(1)}, f32[128,448]{1,0:T(8,128)S(1)}, u32[]{:S(2)}, u32[]{:S(2)}) collective-permute-start(f32[128,448]{1,0:T(8,128)S(1)} %bitcast_add_fusion.16), channel_id=1, source_target_pairs={{256,192},{320,256},{384,320},{448,384},{257,193},{321,257},{385,3... | collective-permute-start | bytes 688136 | tf_op jit(solution)/shard_map/ppermute | solution.py:42
  112.2 5.8 %collective-permute-start.23 = (f32[128,448]{1,0:T(8,128)S(1)}, f32[128,448]{1,0:T(8,128)S(1)}, u32[]{:S(2)}, u32[]{:S(2)}) collective-permute-start(f32[128,448]{1,0:T(8,128)S(1)} %bitcast_add_fusion.3), channel_id=1, source_target_pairs={{256,192},{320,256},{384,320},{448,384},{257,193},{321,257},{385,3... | collective-permute-start | bytes 688136 | tf_op jit(solution)/shard_map/ppermute | solution.py:42
  119.3 2.4 %collective-permute-done.7 = f32[128,448]{1,0:T(8,128)S(1)} collective-permute-done((f32[128,448]{1,0:T(8,128)S(1)}, f32[128,448]{1,0:T(8,128)S(1)}, u32[]{:S(2)}, u32[]{:S(2)}) %collective-permute-start.7) | collective-permute-done | bytes 229408 | tf_op jit(solution)/shard_map/ppermute | solution.py:41
  121.7 3.4 %collective-permute-start.10 = (f32[128,448]{1,0:T(8,128)S(1)}, f32[128,448]{1,0:T(8,128)S(1)}, u32[]{:S(2)}, u32[]{:S(2)}) collective-permute-start(f32[128,448]{1,0:T(8,128)S(1)} %bitcast_add_fusion.15), channel_id=1, source_target_pairs={{192,128},{256,192},{320,256},{384,320},{448,384},{193,129},{257,1... | collective-permute-start | bytes 688136 | tf_op jit(solution)/shard_map/ppermute | solution.py:42
  125.2 2.4 %collective-permute-start.9 = (f32[128,448]{1,0:T(8,128)S(1)}, f32[128,448]{1,0:T(8,128)S(1)}, u32[]{:S(2)}, u32[]{:S(2)}) collective-permute-start(f32[128,448]{1,0:T(8,128)S(1)} %bitcast_add_fusion.22), channel_id=1, source_target_pairs={{0,64},{64,128},{128,192},{192,256},{256,320},{1,65},{65,129},{129... | collective-permute-start | bytes 688136 | tf_op jit(solution)/shard_map/ppermute | solution.py:41
  128.4 4.0 %collective-permute-start.25 = (f32[128,448]{1,0:T(8,128)S(1)}, f32[128,448]{1,0:T(8,128)S(1)}, u32[]{:S(2)}, u32[]{:S(2)}) collective-permute-start(f32[128,448]{1,0:T(8,128)S(1)} %bitcast_add_fusion.2), channel_id=1, source_target_pairs={{192,128},{256,192},{320,256},{384,320},{448,384},{193,129},{257,1... | collective-permute-start | bytes 688136 | tf_op jit(solution)/shard_map/ppermute | solution.py:42
  132.4 1.9 %collective-permute-start.24 = (f32[128,448]{1,0:T(8,128)S(1)}, f32[128,448]{1,0:T(8,128)S(1)}, u32[]{:S(2)}, u32[]{:S(2)}) collective-permute-start(f32[128,448]{1,0:T(8,128)S(1)} %bitcast_add_fusion.9), channel_id=1, source_target_pairs={{0,64},{64,128},{128,192},{192,256},{256,320},{1,65},{65,129},{129... | collective-permute-start | bytes 688136 | tf_op jit(solution)/shard_map/ppermute | solution.py:41
  135.0 4.5 %collective-permute-start.12 = (f32[128,448]{1,0:T(8,128)S(1)}, f32[128,448]{1,0:T(8,128)S(1)}, u32[]{:S(2)}, u32[]{:S(2)}) collective-permute-start(f32[128,448]{1,0:T(8,128)S(1)} %bitcast_add_fusion.14), channel_id=1, source_target_pairs={{128,64},{192,128},{256,192},{320,256},{384,320},{448,384},{129,65... | collective-permute-start | bytes 688136 | tf_op jit(solution)/shard_map/ppermute | solution.py:42
  141.9 4.8 %collective-permute-start.27 = (f32[128,448]{1,0:T(8,128)S(1)}, f32[128,448]{1,0:T(8,128)S(1)}, u32[]{:S(2)}, u32[]{:S(2)}) collective-permute-start(f32[128,448]{1,0:T(8,128)S(1)} %bitcast_add_fusion.1), channel_id=1, source_target_pairs={{128,64},{192,128},{256,192},{320,256},{384,320},{448,384},{129,65... | collective-permute-start | bytes 688136 | tf_op jit(solution)/shard_map/ppermute | solution.py:42
  146.7 1.9 %collective-permute-start.26 = (f32[128,448]{1,0:T(8,128)S(1)}, f32[128,448]{1,0:T(8,128)S(1)}, u32[]{:S(2)}, u32[]{:S(2)}) collective-permute-start(f32[128,448]{1,0:T(8,128)S(1)} %bitcast_add_fusion.10), channel_id=1, source_target_pairs={{0,64},{64,128},{128,192},{192,256},{256,320},{320,384},{1,65},{65... | collective-permute-start | bytes 688136 | tf_op jit(solution)/shard_map/ppermute | solution.py:41
  149.1 4.8 %collective-permute-start.14 = (f32[128,448]{1,0:T(8,128)S(1)}, f32[128,448]{1,0:T(8,128)S(1)}, u32[]{:S(2)}, u32[]{:S(2)}) collective-permute-start(f32[128,448]{1,0:T(8,128)S(1)} %bitcast_add_fusion.13), channel_id=1, source_target_pairs={{64,0},{128,64},{192,128},{256,192},{320,256},{384,320},{448,384},... | collective-permute-start | bytes 688136 | tf_op jit(solution)/shard_map/ppermute | solution.py:42
  153.9 1.9 %collective-permute-start.13 = (f32[128,448]{1,0:T(8,128)S(1)}, f32[128,448]{1,0:T(8,128)S(1)}, u32[]{:S(2)}, u32[]{:S(2)}) collective-permute-start(f32[128,448]{1,0:T(8,128)S(1)} %bitcast_add_fusion.24), channel_id=1, source_target_pairs={{0,64},{64,128},{128,192},{192,256},{256,320},{320,384},{384,448},... | collective-permute-start | bytes 688136 | tf_op jit(solution)/shard_map/ppermute | solution.py:41
  156.3 4.8 %collective-permute-start.29 = (f32[128,448]{1,0:T(8,128)S(1)}, f32[128,448]{1,0:T(8,128)S(1)}, u32[]{:S(2)}, u32[]{:S(2)}) collective-permute-start(f32[128,448]{1,0:T(8,128)S(1)} %bitcast_add_fusion), channel_id=1, source_target_pairs={{64,0},{128,64},{192,128},{256,192},{320,256},{384,320},{448,384},... | collective-permute-start | bytes 688136 | tf_op jit(solution)/shard_map/ppermute | solution.py:42
  161.1 1.9 %collective-permute-start.28 = (f32[128,448]{1,0:T(8,128)S(1)}, f32[128,448]{1,0:T(8,128)S(1)}, u32[]{:S(2)}, u32[]{:S(2)}) collective-permute-start(f32[128,448]{1,0:T(8,128)S(1)} %bitcast_add_fusion.11), channel_id=1, source_target_pairs={{0,64},{64,128},{128,192},{192,256},{256,320},{320,384},{384,448},... | collective-permute-start | bytes 688136 | tf_op jit(solution)/shard_map/ppermute | solution.py:41
  164.9 5.7 %collective-permute-done.28 = f32[128,448]{1,0:T(8,128)S(1)} collective-permute-done((f32[128,448]{1,0:T(8,128)S(1)}, f32[128,448]{1,0:T(8,128)S(1)}, u32[]{:S(2)}, u32[]{:S(2)}) %collective-permute-start.28) | collective-permute-done | bytes 229408 | tf_op jit(solution)/shard_map/ppermute | solution.py:41
  (79 shorter events, 25.4 us)
Async XLA Ops:
  10.6 28.4 %all-to-all-start.1 = ((bf16[16,32,256]{2,1,0:T(8,128)(2,1)}), bf16[16,32,256]{2,1,0:T(8,128)(2,1)S(1)}, u32[]{:S(2)}, u32[]{:S(2)}) async-start(bf16[16,32,256]{2,1,0:T(8,128)(2,1)} %pad_maximum_fusion), calls=%async_computation.1 | async-start | bytes 524288 | tf_op jit(solution)/shard_map/all_to_all | solution.py:17
  40.7 30.8 %all-to-all-start.2 = ((bf16[16,8,32,256]{3,2,1,0:T(8,128)(2,1)}), bf16[16,8,32,256]{3,2,1,0:T(8,128)(2,1)S(1)}, u32[]{:S(2)}, u32[]{:S(2)}) async-start(bf16[16,8,32,256]{3,2,1,0:T(8,128)(2,1)} %broadcast_in_dim.2), calls=%async_computation.2 | async-start | bytes 4194304 | tf_op jit(solution)/shard_map/all_to_all | solution.py:19
  46.2 25.6 %collective-permute-start = (bf16[448,512]{1,0:T(8,128)(2,1)S(1)}, bf16[448,512]{1,0:T(8,128)(2,1)}, u32[]{:S(2)}, u32[]{:S(2)}) collective-permute-start(bf16[448,512]{1,0:T(8,128)(2,1)S(1)} %bitcast.94), channel_id=1, source_target_pairs={{0,32},{32,0},{1,33},{33,1},{2,34},{34,2},{3,35},{35,3},{4,36},{36... | collective-permute-start | bytes 1376264 | tf_op jit(solution)/shard_map/ppermute | solution.py:14
  48.1 28.3 %collective-permute-start.15 = (bf16[448,512]{1,0:T(8,128)(2,1)S(1)}, bf16[448,512]{1,0:T(8,128)(2,1)S(1)}, u32[]{:S(2)}, u32[]{:S(2)}) collective-permute-start(bf16[448,512]{1,0:T(8,128)(2,1)S(1)} %bitcast.96), channel_id=1, source_target_pairs={{0,32},{32,0},{1,33},{33,1},{2,34},{34,2},{3,35},{35,3},{4,36},{36... | collective-permute-start | bytes 1376264 | tf_op jit(solution)/shard_map/ppermute | solution.py:14
  82.9 22.2 %collective-permute-start.6 = (f32[128,448]{1,0:T(8,128)S(1)}, f32[128,448]{1,0:T(8,128)S(1)}, u32[]{:S(2)}, u32[]{:S(2)}) collective-permute-start(f32[128,448]{1,0:T(8,128)S(1)} %bitcast_add_fusion.17), channel_id=1, source_target_pairs={{320,256},{384,320},{448,384},{321,257},{385,321},{449,385},{322,2... | collective-permute-start | bytes 688136 | tf_op jit(solution)/shard_map/ppermute | solution.py:42
  84.2 20.9 %collective-permute-start.5 = (f32[128,448]{1,0:T(8,128)S(1)}, f32[128,448]{1,0:T(8,128)S(1)}, u32[]{:S(2)}, u32[]{:S(2)}) collective-permute-start(f32[128,448]{1,0:T(8,128)S(1)} %bitcast_add_fusion.20), channel_id=1, source_target_pairs={{0,64},{64,128},{128,192},{1,65},{65,129},{129,193},{2,66},{66,130... | collective-permute-start | bytes 688136 | tf_op jit(solution)/shard_map/ppermute | solution.py:41
  85.0 27.2 %collective-permute-start.21 = (f32[128,448]{1,0:T(8,128)S(1)}, f32[128,448]{1,0:T(8,128)S(1)}, u32[]{:S(2)}, u32[]{:S(2)}) collective-permute-start(f32[128,448]{1,0:T(8,128)S(1)} %bitcast_add_fusion.4), channel_id=1, source_target_pairs={{320,256},{384,320},{448,384},{321,257},{385,321},{449,385},{322,2... | collective-permute-start | bytes 688136 | tf_op jit(solution)/shard_map/ppermute | solution.py:42
  86.3 25.8 %collective-permute-start.20 = (f32[128,448]{1,0:T(8,128)S(1)}, f32[128,448]{1,0:T(8,128)S(1)}, u32[]{:S(2)}, u32[]{:S(2)}) collective-permute-start(f32[128,448]{1,0:T(8,128)S(1)} %bitcast_add_fusion.7), channel_id=1, source_target_pairs={{0,64},{64,128},{128,192},{1,65},{65,129},{129,193},{2,66},{66,130... | collective-permute-start | bytes 688136 | tf_op jit(solution)/shard_map/ppermute | solution.py:41
  105.1 14.2 %collective-permute-start.8 = (f32[128,448]{1,0:T(8,128)S(1)}, f32[128,448]{1,0:T(8,128)S(1)}, u32[]{:S(2)}, u32[]{:S(2)}) collective-permute-start(f32[128,448]{1,0:T(8,128)S(1)} %bitcast_add_fusion.16), channel_id=1, source_target_pairs={{256,192},{320,256},{384,320},{448,384},{257,193},{321,257},{385,3... | collective-permute-start | bytes 688136 | tf_op jit(solution)/shard_map/ppermute | solution.py:42
  110.8 10.9 %collective-permute-start.7 = (f32[128,448]{1,0:T(8,128)S(1)}, f32[128,448]{1,0:T(8,128)S(1)}, u32[]{:S(2)}, u32[]{:S(2)}) collective-permute-start(f32[128,448]{1,0:T(8,128)S(1)} %bitcast_add_fusion.21), channel_id=1, source_target_pairs={{0,64},{64,128},{128,192},{192,256},{1,65},{65,129},{129,193},{193... | collective-permute-start | bytes 688136 | tf_op jit(solution)/shard_map/ppermute | solution.py:41
  112.2 15.4 %collective-permute-start.23 = (f32[128,448]{1,0:T(8,128)S(1)}, f32[128,448]{1,0:T(8,128)S(1)}, u32[]{:S(2)}, u32[]{:S(2)}) collective-permute-start(f32[128,448]{1,0:T(8,128)S(1)} %bitcast_add_fusion.3), channel_id=1, source_target_pairs={{256,192},{320,256},{384,320},{448,384},{257,193},{321,257},{385,3... | collective-permute-start | bytes 688136 | tf_op jit(solution)/shard_map/ppermute | solution.py:42
  118.0 10.3 %collective-permute-start.22 = (f32[128,448]{1,0:T(8,128)S(1)}, f32[128,448]{1,0:T(8,128)S(1)}, u32[]{:S(2)}, u32[]{:S(2)}) collective-permute-start(f32[128,448]{1,0:T(8,128)S(1)} %bitcast_add_fusion.8), channel_id=1, source_target_pairs={{0,64},{64,128},{128,192},{192,256},{1,65},{65,129},{129,193},{193... | collective-permute-start | bytes 688136 | tf_op jit(solution)/shard_map/ppermute | solution.py:41
  121.7 12.6 %collective-permute-start.10 = (f32[128,448]{1,0:T(8,128)S(1)}, f32[128,448]{1,0:T(8,128)S(1)}, u32[]{:S(2)}, u32[]{:S(2)}) collective-permute-start(f32[128,448]{1,0:T(8,128)S(1)} %bitcast_add_fusion.15), channel_id=1, source_target_pairs={{192,128},{256,192},{320,256},{384,320},{448,384},{193,129},{257,1... | collective-permute-start | bytes 688136 | tf_op jit(solution)/shard_map/ppermute | solution.py:42
  125.2 9.7 %collective-permute-start.9 = (f32[128,448]{1,0:T(8,128)S(1)}, f32[128,448]{1,0:T(8,128)S(1)}, u32[]{:S(2)}, u32[]{:S(2)}) collective-permute-start(f32[128,448]{1,0:T(8,128)S(1)} %bitcast_add_fusion.22), channel_id=1, source_target_pairs={{0,64},{64,128},{128,192},{192,256},{256,320},{1,65},{65,129},{129... | collective-permute-start | bytes 688136 | tf_op jit(solution)/shard_map/ppermute | solution.py:41
  128.4 13.1 %collective-permute-start.25 = (f32[128,448]{1,0:T(8,128)S(1)}, f32[128,448]{1,0:T(8,128)S(1)}, u32[]{:S(2)}, u32[]{:S(2)}) collective-permute-start(f32[128,448]{1,0:T(8,128)S(1)} %bitcast_add_fusion.2), channel_id=1, source_target_pairs={{192,128},{256,192},{320,256},{384,320},{448,384},{193,129},{257,1... | collective-permute-start | bytes 688136 | tf_op jit(solution)/shard_map/ppermute | solution.py:42
  132.4 9.5 %collective-permute-start.24 = (f32[128,448]{1,0:T(8,128)S(1)}, f32[128,448]{1,0:T(8,128)S(1)}, u32[]{:S(2)}, u32[]{:S(2)}) collective-permute-start(f32[128,448]{1,0:T(8,128)S(1)} %bitcast_add_fusion.9), channel_id=1, source_target_pairs={{0,64},{64,128},{128,192},{192,256},{256,320},{1,65},{65,129},{129... | collective-permute-start | bytes 688136 | tf_op jit(solution)/shard_map/ppermute | solution.py:41
  135.0 13.7 %collective-permute-start.12 = (f32[128,448]{1,0:T(8,128)S(1)}, f32[128,448]{1,0:T(8,128)S(1)}, u32[]{:S(2)}, u32[]{:S(2)}) collective-permute-start(f32[128,448]{1,0:T(8,128)S(1)} %bitcast_add_fusion.14), channel_id=1, source_target_pairs={{128,64},{192,128},{256,192},{320,256},{384,320},{448,384},{129,65... | collective-permute-start | bytes 688136 | tf_op jit(solution)/shard_map/ppermute | solution.py:42
  139.6 9.5 %collective-permute-start.11 = (f32[128,448]{1,0:T(8,128)S(1)}, f32[128,448]{1,0:T(8,128)S(1)}, u32[]{:S(2)}, u32[]{:S(2)}) collective-permute-start(f32[128,448]{1,0:T(8,128)S(1)} %bitcast_add_fusion.23), channel_id=1, source_target_pairs={{0,64},{64,128},{128,192},{192,256},{256,320},{320,384},{1,65},{65... | collective-permute-start | bytes 688136 | tf_op jit(solution)/shard_map/ppermute | solution.py:41
  141.9 14.0 %collective-permute-start.27 = (f32[128,448]{1,0:T(8,128)S(1)}, f32[128,448]{1,0:T(8,128)S(1)}, u32[]{:S(2)}, u32[]{:S(2)}) collective-permute-start(f32[128,448]{1,0:T(8,128)S(1)} %bitcast_add_fusion.1), channel_id=1, source_target_pairs={{128,64},{192,128},{256,192},{320,256},{384,320},{448,384},{129,65... | collective-permute-start | bytes 688136 | tf_op jit(solution)/shard_map/ppermute | solution.py:42
  146.7 9.5 %collective-permute-start.26 = (f32[128,448]{1,0:T(8,128)S(1)}, f32[128,448]{1,0:T(8,128)S(1)}, u32[]{:S(2)}, u32[]{:S(2)}) collective-permute-start(f32[128,448]{1,0:T(8,128)S(1)} %bitcast_add_fusion.10), channel_id=1, source_target_pairs={{0,64},{64,128},{128,192},{192,256},{256,320},{320,384},{1,65},{65... | collective-permute-start | bytes 688136 | tf_op jit(solution)/shard_map/ppermute | solution.py:41
  149.1 14.0 %collective-permute-start.14 = (f32[128,448]{1,0:T(8,128)S(1)}, f32[128,448]{1,0:T(8,128)S(1)}, u32[]{:S(2)}, u32[]{:S(2)}) collective-permute-start(f32[128,448]{1,0:T(8,128)S(1)} %bitcast_add_fusion.13), channel_id=1, source_target_pairs={{64,0},{128,64},{192,128},{256,192},{320,256},{384,320},{448,384},... | collective-permute-start | bytes 688136 | tf_op jit(solution)/shard_map/ppermute | solution.py:42
  153.9 9.5 %collective-permute-start.13 = (f32[128,448]{1,0:T(8,128)S(1)}, f32[128,448]{1,0:T(8,128)S(1)}, u32[]{:S(2)}, u32[]{:S(2)}) collective-permute-start(f32[128,448]{1,0:T(8,128)S(1)} %bitcast_add_fusion.24), channel_id=1, source_target_pairs={{0,64},{64,128},{128,192},{192,256},{256,320},{320,384},{384,448},... | collective-permute-start | bytes 688136 | tf_op jit(solution)/shard_map/ppermute | solution.py:41
  156.3 8.7 %collective-permute-start.29 = (f32[128,448]{1,0:T(8,128)S(1)}, f32[128,448]{1,0:T(8,128)S(1)}, u32[]{:S(2)}, u32[]{:S(2)}) collective-permute-start(f32[128,448]{1,0:T(8,128)S(1)} %bitcast_add_fusion), channel_id=1, source_target_pairs={{64,0},{128,64},{192,128},{256,192},{320,256},{384,320},{448,384},... | collective-permute-start | bytes 688136 | tf_op jit(solution)/shard_map/ppermute | solution.py:42
  161.1 9.5 %collective-permute-start.28 = (f32[128,448]{1,0:T(8,128)S(1)}, f32[128,448]{1,0:T(8,128)S(1)}, u32[]{:S(2)}, u32[]{:S(2)}) collective-permute-start(f32[128,448]{1,0:T(8,128)S(1)} %bitcast_add_fusion.11), channel_id=1, source_target_pairs={{0,64},{64,128},{128,192},{192,256},{256,320},{320,384},{384,448},... | collective-permute-start | bytes 688136 | tf_op jit(solution)/shard_map/ppermute | solution.py:41
  (10 other events, 38.3 us)

commit v2 on v0

v2 whole, which is shorter than its diff:
```python
import jax
import jax.numpy as jnp
from jax import lax
from jax.sharding import Mesh, PartitionSpec as P

F32 = jnp.float32
AXES = ("h", "i", "q", "zh", "x", "y")
SIZES = (2, 4, 2, 2, 4, 4)
SWAP = [(0, 1), (1, 0)]
RING = [(j, (j + 1) % 4) for j in range(4)]


def body(tokens, gate_weight, up_weight):
    h, i, q, zh = (lax.axis_index(a) for a in ("h", "i", "q", "zh"))
    units = [[gate_weight.T], [up_weight.T]]
    for _ in range(3):
        for k in range(2):
            units[k].append(lax.ppermute(units[k][-1], "i", RING))

    far = lax.ppermute(tokens, ("h", "zh"), [(0, 1), (2, 0), (1, 3), (3, 2)])
    near = lax.ppermute(tokens, ("h", "zh"), [(2, 1), (1, 2)])
    near = jnp.where(h == zh, tokens, near)
    two = jnp.where(zh == 0, jnp.stack([near, far]), jnp.stack([far, near]))
    whole = lax.all_to_all(jnp.broadcast_to(two[None], (16, 2, 128, 256)), ("x", "y"), 0, 0, tiled=True)
    whole = whole.reshape(4, 2, 2, 256, 256)
    mine = lax.dynamic_index_in_dim(whole, q, 1, False)
    theirs = lax.ppermute(lax.dynamic_index_in_dim(whole, 1 - q, 1, False), "q", SWAP)
    mine, theirs = (t.transpose(0, 2, 1, 3).reshape(4, 256, 512) for t in (mine, theirs))

    last = (i + 1) & 3

    def dot(t, u, k):
        at = last if u == 3 else (i - u) & 3
        t = lax.dynamic_index_in_dim(t, at, 0, False)
        return lax.dot_general(t, units[k][u], (((1,), (1,)), ((), ())), preferred_element_type=F32)

    both = []
    for k in range(2):
        sent = lax.ppermute(sum(dot(theirs, u, k) for u in range(4)), "q", SWAP)
        total = sum(dot(mine, u, k) for u in range(4)) + sent
        if k:
            total, _ = lax.optimization_barrier((total, away))
        total = total.reshape(2, 128, 448)
        away = (16 * lax.dynamic_index_in_dim(total, 1 - h, 0, False)).astype(jnp.float16)
        keep = lax.dynamic_index_in_dim(total, h, 0, False)
        come = lax.ppermute(away, "h", SWAP)
        both.append(keep + come.astype(F32) / 16)
    gate, up = both
    return (jax.nn.silu(gate) * up).astype(jnp.bfloat16)


def solution(mesh):
    fine = Mesh(mesh.devices.reshape(SIZES), AXES)
    spec = P(("h", "i", "q"), ("zh", "x", "y"))
    return jax.shard_map(body, mesh=fine, in_specs=(spec,) * 3, out_specs=spec, check_vma=False)
```

time: 390 us -> 142 us (0.36)
  the two profiles are of different devices: /device:TPU:4 before, /device:TPU:1 now
where the time goes in v2:
time: 142 us; the launch traced here: 141 us
  starting transfers between devices  72.1 us (51%)
  waiting for transfers between devices  45.3 us (32%)
  matrix products  14.8 us (10%)
  local copies, waits for them, and re-layouts  7.07 us (5%)
  other arithmetic  1.7 us (1%)
    ppermute x6, waiting for transfers between devices, body(): units[k].append(lax.ppermute(units[k][-1], 'i', RING))  23.6 us
    ppermute x6, starting transfers between devices, body(): units[k].append(lax.ppermute(units[k][-1], 'i', RING))  22.8 us
    ppermute x2, waiting for transfers between devices, body(): come = lax.ppermute(away, 'h', SWAP)  17.9 us
    ppermute x1, starting transfers between devices, body(): far = lax.ppermute(tokens, ('h', 'zh'), [(0, 1), (2, 0), (1, 3), (3, 2)])  17.5 us
    dot_general x16, matrix products, dot(): lax.dot_general(t, units[k][u], (((1,), (1,)), ((), ())), preferred_eleme...  14.8 us
    ppermute x2, starting transfers between devices, body(): come = lax.ppermute(away, 'h', SWAP)  12.3 us
    ppermute x1, starting transfers between devices, body(): lax.ppermute(lax.dynamic_index_in_dim(whole, 1 - q, 1, False), 'q', SWAP)  7.59 us
    all_to_all x1, starting transfers between devices, body(): lax.all_to_all(jnp.broadcast_to(two[None], (16, 2, 128, 256)), ('x', 'y')...  6.89 us
  transfers between devices with their start and end apart: 14, of which 7 were waited for; matrix products, arithmetic and copies ran while one was open for 13% of the time, Pallas kernels for 0%

profile of v2, /device:TPU:1, one launch (start us, length us, event | category | flops | bytes accessed | tf_op | source)
XLA Modules:
  0.0 141.5 jit_solution(16992274741560305241)
XLA Ops:
  0.7 17.5 %collective-permute-start.1 = (bf16[128,256]{1,0:T(8,128)(2,1)}, bf16[128,256]{1,0:T(8,128)(2,1)S(1)}, u32[]{:S(2)}, u32[]{:S(2)}) collective-permute-start(bf16[128,256]{1,0:T(8,128)(2,1)} %param.3), channel_id=1, source_target_pairs={{0,16},{256,0},{16,272},{272,256},{1,17},{257,1},{17,273},{273,257... | collective-permute-start | bytes 196616 | tf_op jit(solution)/shard_map/ppermute | solution.py:20
  19.1 3.8 %collective-permute-done.1 = bf16[128,256]{1,0:T(8,128)(2,1)S(1)} collective-permute-done((bf16[128,256]{1,0:T(8,128)(2,1)}, bf16[128,256]{1,0:T(8,128)(2,1)S(1)}, u32[]{:S(2)}, u32[]{:S(2)}) %collective-permute-start.1) | collective-permute-done | bytes 65568 | tf_op jit(solution)/shard_map/ppermute | solution.py:20
  22.9 1.6 %broadcast_in_dim.2 = bf16[16,2,128,256]{3,2,1,0:T(8,128)(2,1)} broadcast(bf16[2,128,256]{2,1,0:T(8,128)(2,1)S(1)} %maximum_select_fusion), dimensions={1,2,3} | broadcast | bytes 2228224 | tf_op jit(solution)/shard_map/broadcast_in_dim | solution.py:24
  24.5 6.9 %all-to-all-start = ((bf16[16,2,128,256]{3,2,1,0:T(8,128)(2,1)}), bf16[16,2,128,256]{3,2,1,0:T(8,128)(2,1)S(1)}, u32[]{:S(2)}, u32[]{:S(2)}) async-start(bf16[16,2,128,256]{3,2,1,0:T(8,128)(2,1)} %broadcast_in_dim.2), calls=%async_computation | async-start | bytes 4194304 | tf_op jit(solution)/shard_map/all_to_all | solution.py:24
  31.4 4.2 %collective-permute-start.2 = (bf16[448,512]{1,0:T(8,128)(2,1)S(1)}, bf16[448,512]{1,0:T(8,128)(2,1)}, u32[]{:S(2)}, u32[]{:S(2)}) collective-permute-start(bf16[448,512]{1,0:T(8,128)(2,1)S(1)} %bitcast.100), channel_id=1, source_target_pairs={{0,64},{64,128},{128,192},{192,0},{1,65},{65,129},{129,193},{193,1... | collective-permute-start | bytes 1376264 | tf_op jit(solution)/shard_map/ppermute | solution.py:18
  35.6 1.9 %collective-permute-start.8 = (bf16[448,512]{1,0:T(8,128)(2,1)S(1)}, bf16[448,512]{1,0:T(8,128)(2,1)S(1)}, u32[]{:S(2)}, u32[]{:S(2)}) collective-permute-start(bf16[448,512]{1,0:T(8,128)(2,1)S(1)} %bitcast.101), channel_id=1, source_target_pairs={{0,64},{64,128},{128,192},{192,0},{1,65},{65,129},{129,193},{193,1... | collective-permute-start | bytes 1376264 | tf_op jit(solution)/shard_map/ppermute | solution.py:18
  37.5 6.6 %collective-permute-done.2 = bf16[448,512]{1,0:T(8,128)(2,1)} collective-permute-done((bf16[448,512]{1,0:T(8,128)(2,1)S(1)}, bf16[448,512]{1,0:T(8,128)(2,1)}, u32[]{:S(2)}, u32[]{:S(2)}) %collective-permute-start.2) | collective-permute-done | bytes 458784 | tf_op jit(solution)/shard_map/ppermute | solution.py:18
  44.1 4.2 %collective-permute-start.3 = (bf16[448,512]{1,0:T(8,128)(2,1)}, bf16[448,512]{1,0:T(8,128)(2,1)}, u32[]{:S(2)}, u32[]{:S(2)}) collective-permute-start(bf16[448,512]{1,0:T(8,128)(2,1)} %collective-permute-done.2), channel_id=1, source_target_pairs={{0,64},{64,128},{128,192},{192,0},{1,65},{65,129},{129,193},{193,1... | collective-permute-start | bytes 1376264 | tf_op jit(solution)/shard_map/ppermute | solution.py:18
  48.3 5.6 %collective-permute-done.8 = bf16[448,512]{1,0:T(8,128)(2,1)S(1)} collective-permute-done((bf16[448,512]{1,0:T(8,128)(2,1)S(1)}, bf16[448,512]{1,0:T(8,128)(2,1)S(1)}, u32[]{:S(2)}, u32[]{:S(2)}) %collective-permute-start.8) | collective-permute-done | bytes 458784 | tf_op jit(solution)/shard_map/ppermute | solution.py:18
  54.0 4.1 %collective-permute-start.9 = (bf16[448,512]{1,0:T(8,128)(2,1)S(1)}, bf16[448,512]{1,0:T(8,128)(2,1)}, u32[]{:S(2)}, u32[]{:S(2)}) collective-permute-start(bf16[448,512]{1,0:T(8,128)(2,1)S(1)} %collective-permute-done.8), channel_id=1, source_target_pairs={{0,64},{64,128},{128,192},{192,0},{1,65},{65,129},{129,193},{193,1... | collective-permute-start | bytes 1376264 | tf_op jit(solution)/shard_map/ppermute | solution.py:18
  58.1 5.8 %collective-permute-done.3 = bf16[448,512]{1,0:T(8,128)(2,1)} collective-permute-done((bf16[448,512]{1,0:T(8,128)(2,1)}, bf16[448,512]{1,0:T(8,128)(2,1)}, u32[]{:S(2)}, u32[]{:S(2)}) %collective-permute-start.3) | collective-permute-done | bytes 458784 | tf_op jit(solution)/shard_map/ppermute | solution.py:18
  63.9 4.1 %collective-permute-start.4 = (bf16[448,512]{1,0:T(8,128)(2,1)}, bf16[448,512]{1,0:T(8,128)(2,1)}, u32[]{:S(2)}, u32[]{:S(2)}) collective-permute-start(bf16[448,512]{1,0:T(8,128)(2,1)} %collective-permute-done.3), channel_id=1, source_target_pairs={{0,64},{64,128},{128,192},{192,0},{1,65},{65,129},{129,193},{193,1... | collective-permute-start | bytes 1376264 | tf_op jit(solution)/shard_map/ppermute | solution.py:18
  68.0 5.6 %collective-permute-done.9 = bf16[448,512]{1,0:T(8,128)(2,1)} collective-permute-done((bf16[448,512]{1,0:T(8,128)(2,1)S(1)}, bf16[448,512]{1,0:T(8,128)(2,1)}, u32[]{:S(2)}, u32[]{:S(2)}) %collective-permute-start.9) | collective-permute-done | bytes 458784 | tf_op jit(solution)/shard_map/ppermute | solution.py:18
  73.6 4.2 %collective-permute-start.10 = (bf16[448,512]{1,0:T(8,128)(2,1)}, bf16[448,512]{1,0:T(8,128)(2,1)}, u32[]{:S(2)}, u32[]{:S(2)}) collective-permute-start(bf16[448,512]{1,0:T(8,128)(2,1)} %collective-permute-done.9), channel_id=1, source_target_pairs={{0,64},{64,128},{128,192},{192,0},{1,65},{65,129},{129,193},{193,1... | collective-permute-start | bytes 1376264 | tf_op jit(solution)/shard_map/ppermute | solution.py:18
  79.6 7.6 %collective-permute-start.5 = (bf16[4,2,256,256]{3,2,1,0:T(8,128)(2,1)}, bf16[4,2,256,256]{3,2,1,0:T(8,128)(2,1)S(1)}, u32[]{:S(2)}, u32[]{:S(2)}) collective-permute-start(bf16[4,2,256,256]{3,2,1,0:T(8,128)(2,1)} %get-tuple-element.8), channel_id=1, source_target_pairs={{0,32},{32,0},{1,33},{33,1},{2,34},{34,2},{3,35},{35,3},{4,36},{36... | collective-permute-start | bytes 3145736 | tf_op jit(solution)/shard_map/ppermute | solution.py:27
  89.4 1.3 convolution_add_fusion.10
  90.7 1.4 convolution_add_fusion.4
  93.1 1.5 %copy.11 = bf16[4,256,2,256]{1,3,2,0:T(8,128)(2,1)S(1)} copy(bf16[4,256,2,256]{3,1,2,0:T(8,128)(2,1)} %bitcast.102) | data formatting | bytes 2097152 | tf_op jit(solution)/shard_map/transpose | solution.py:28
  99.2 1.9 %collective-permute-start.6 = (f32[256,448]{0,1:T(8,128)S(1)}, f32[256,448]{0,1:T(8,128)S(1)}, u32[]{:S(2)}, u32[]{:S(2)}) collective-permute-start(f32[256,448]{0,1:T(8,128)S(1)} %convolution_add_fusion.6), channel_id=1, source_target_pairs={{0,32},{32,0},{1,33},{33,1},{2,34},{34,2},{3,35},{35,3},{4,36},{36... | collective-permute-start | bytes 1376264 | tf_op jit(solution)/shard_map/ppermute | solution.py:39
  104.0 2.4 %collective-permute-start.11 = (f32[256,448]{0,1:T(8,128)S(1)}, f32[256,448]{0,1:T(8,128)S(1)}, u32[]{:S(2)}, u32[]{:S(2)}) collective-permute-start(f32[256,448]{0,1:T(8,128)S(1)} %convolution_add_fusion), channel_id=1, source_target_pairs={{0,32},{32,0},{1,33},{33,1},{2,34},{34,2},{3,35},{35,3},{4,36},{36... | collective-permute-start | bytes 1376264 | tf_op jit(solution)/shard_map/ppermute | solution.py:39
  110.5 10.4 %collective-permute-start.12 = (f16[128,448]{0,1:T(8,128)(2,1)S(1)}, f16[128,448]{0,1:T(8,128)(2,1)S(1)}, u32[]{:S(2)}, u32[]{:S(2)}) collective-permute-start(f16[128,448]{0,1:T(8,128)(2,1)S(1)} %fusion.39), channel_id=1, source_target_pairs={{0,256},{256,0},{1,257},{257,1},{2,258},{258,2},{3,259},{259,3},{4... | collective-permute-start | bytes 344072 | tf_op jit(solution)/shard_map/ppermute | solution.py:46
  120.9 1.9 %collective-permute-start.7 = (f16[128,448]{0,1:T(8,128)(2,1)S(1)}, f16[128,448]{0,1:T(8,128)(2,1)S(1)}, u32[]{:S(2)}, u32[]{:S(2)}) collective-permute-start(f16[128,448]{0,1:T(8,128)(2,1)S(1)} %fusion.38), channel_id=1, source_target_pairs={{0,256},{256,0},{1,257},{257,1},{2,258},{258,2},{3,259},{259,3},{4... | collective-permute-start | bytes 344072 | tf_op jit(solution)/shard_map/ppermute | solution.py:46
  122.8 15.4 %collective-permute-done.12 = f16[128,448]{0,1:T(8,128)(2,1)S(1)} collective-permute-done((f16[128,448]{0,1:T(8,128)(2,1)S(1)}, f16[128,448]{0,1:T(8,128)(2,1)S(1)}, u32[]{:S(2)}, u32[]{:S(2)}) %collective-permute-start.12) | collective-permute-done | bytes 114720 | tf_op jit(solution)/shard_map/ppermute | solution.py:46
  138.3 2.5 %collective-permute-done.7 = f16[128,448]{0,1:T(8,128)(2,1)S(1)} collective-permute-done((f16[128,448]{0,1:T(8,128)(2,1)S(1)}, f16[128,448]{0,1:T(8,128)(2,1)S(1)}, u32[]{:S(2)}, u32[]{:S(2)}) %collective-permute-start.7) | collective-permute-done | bytes 114720 | tf_op jit(solution)/shard_map/ppermute | solution.py:46
  (53 shorter events, 18.5 us)
Async XLA Ops:
  0.0 18.2 %collective-permute-start = (bf16[128,256]{1,0:T(8,128)(2,1)}, bf16[128,256]{1,0:T(8,128)(2,1)S(1)}, u32[]{:S(2)}, u32[]{:S(2)}) collective-permute-start(bf16[128,256]{1,0:T(8,128)(2,1)} %param.3), channel_id=1, source_target_pairs={{256,16},{16,256},{257,17},{17,257},{258,18},{18,258},{259,19},{19... | collective-permute-start | bytes 196616 | tf_op jit(solution)/shard_map/ppermute | solution.py:21
  0.7 22.2 %collective-permute-start.1 = (bf16[128,256]{1,0:T(8,128)(2,1)}, bf16[128,256]{1,0:T(8,128)(2,1)S(1)}, u32[]{:S(2)}, u32[]{:S(2)}) collective-permute-start(bf16[128,256]{1,0:T(8,128)(2,1)} %param.3), channel_id=1, source_target_pairs={{0,16},{256,0},{16,272},{272,256},{1,17},{257,1},{17,273},{273,257... | collective-permute-start | bytes 196616 | tf_op jit(solution)/shard_map/ppermute | solution.py:20
  24.5 6.9 %copy-start = (bf16[512,448]{0,1:T(8,128)(2,1)S(1)}, bf16[512,448]{0,1:T(8,128)(2,1)}, u32[]{:S(2)}) copy-start(bf16[512,448]{0,1:T(8,128)(2,1)} %param.4) | copy-start | bytes 1376260
  24.5 11.1 %copy-start.3 = (bf16[512,448]{0,1:T(8,128)(2,1)S(1)}, bf16[512,448]{0,1:T(8,128)(2,1)}, u32[]{:S(2)}) copy-start(bf16[512,448]{0,1:T(8,128)(2,1)} %param.5) | copy-start | bytes 1376260
  24.5 53.4 %all-to-all-start = ((bf16[16,2,128,256]{3,2,1,0:T(8,128)(2,1)}), bf16[16,2,128,256]{3,2,1,0:T(8,128)(2,1)S(1)}, u32[]{:S(2)}, u32[]{:S(2)}) async-start(bf16[16,2,128,256]{3,2,1,0:T(8,128)(2,1)} %broadcast_in_dim.2), calls=%async_computation | async-start | bytes 4194304 | tf_op jit(solution)/shard_map/all_to_all | solution.py:24
  31.4 12.8 %collective-permute-start.2 = (bf16[448,512]{1,0:T(8,128)(2,1)S(1)}, bf16[448,512]{1,0:T(8,128)(2,1)}, u32[]{:S(2)}, u32[]{:S(2)}) collective-permute-start(bf16[448,512]{1,0:T(8,128)(2,1)S(1)} %bitcast.100), channel_id=1, source_target_pairs={{0,64},{64,128},{128,192},{192,0},{1,65},{65,129},{129,193},{193,1... | collective-permute-start | bytes 1376264 | tf_op jit(solution)/shard_map/ppermute | solution.py:18
  35.6 18.3 %collective-permute-start.8 = (bf16[448,512]{1,0:T(8,128)(2,1)S(1)}, bf16[448,512]{1,0:T(8,128)(2,1)S(1)}, u32[]{:S(2)}, u32[]{:S(2)}) collective-permute-start(bf16[448,512]{1,0:T(8,128)(2,1)S(1)} %bitcast.101), channel_id=1, source_target_pairs={{0,64},{64,128},{128,192},{192,0},{1,65},{65,129},{129,193},{193,1... | collective-permute-start | bytes 1376264 | tf_op jit(solution)/shard_map/ppermute | solution.py:18
  44.1 19.8 %collective-permute-start.3 = (bf16[448,512]{1,0:T(8,128)(2,1)}, bf16[448,512]{1,0:T(8,128)(2,1)}, u32[]{:S(2)}, u32[]{:S(2)}) collective-permute-start(bf16[448,512]{1,0:T(8,128)(2,1)} %collective-permute-done.2), channel_id=1, source_target_pairs={{0,64},{64,128},{128,192},{192,0},{1,65},{65,129},{129,193},{193,1... | collective-permute-start | bytes 1376264 | tf_op jit(solution)/shard_map/ppermute | solution.py:18
  54.0 23.9 %copy-start.6 = (bf16[448,512]{1,0:T(8,128)(2,1)}, bf16[448,512]{1,0:T(8,128)(2,1)S(1)}, u32[]{:S(2)}) copy-start(bf16[448,512]{1,0:T(8,128)(2,1)S(1)} %collective-permute-done.8) | copy-start | bytes 1376260
  54.0 19.7 %collective-permute-start.9 = (bf16[448,512]{1,0:T(8,128)(2,1)S(1)}, bf16[448,512]{1,0:T(8,128)(2,1)}, u32[]{:S(2)}, u32[]{:S(2)}) collective-permute-start(bf16[448,512]{1,0:T(8,128)(2,1)S(1)} %collective-permute-done.8), channel_id=1, source_target_pairs={{0,64},{64,128},{128,192},{192,0},{1,65},{65,129},{129,193},{193,1... | collective-permute-start | bytes 1376264 | tf_op jit(solution)/shard_map/ppermute | solution.py:18
  63.9 34.0 %collective-permute-start.4 = (bf16[448,512]{1,0:T(8,128)(2,1)}, bf16[448,512]{1,0:T(8,128)(2,1)}, u32[]{:S(2)}, u32[]{:S(2)}) collective-permute-start(bf16[448,512]{1,0:T(8,128)(2,1)} %collective-permute-done.3), channel_id=1, source_target_pairs={{0,64},{64,128},{128,192},{192,0},{1,65},{65,129},{129,193},{193,1... | collective-permute-start | bytes 1376264 | tf_op jit(solution)/shard_map/ppermute | solution.py:18
  73.6 29.1 %collective-permute-start.10 = (bf16[448,512]{1,0:T(8,128)(2,1)}, bf16[448,512]{1,0:T(8,128)(2,1)}, u32[]{:S(2)}, u32[]{:S(2)}) collective-permute-start(bf16[448,512]{1,0:T(8,128)(2,1)} %collective-permute-done.9), channel_id=1, source_target_pairs={{0,64},{64,128},{128,192},{192,0},{1,65},{65,129},{129,193},{193,1... | collective-permute-start | bytes 1376264 | tf_op jit(solution)/shard_map/ppermute | solution.py:18
  79.1 8.1 %copy-start.1 = (bf16[512,448]{0,1:T(8,128)(2,1)S(1)}, bf16[512,448]{0,1:T(8,128)(2,1)}, u32[]{:S(2)}) copy-start(bf16[512,448]{0,1:T(8,128)(2,1)} %param.4) | copy-start | bytes 1376260
  79.1 8.4 %copy-start.4 = (bf16[512,448]{0,1:T(8,128)(2,1)S(1)}, bf16[512,448]{0,1:T(8,128)(2,1)}, u32[]{:S(2)}) copy-start(bf16[512,448]{0,1:T(8,128)(2,1)} %param.5) | copy-start | bytes 1376260
  79.6 9.5 %copy-start.7 = (bf16[448,512]{1,0:T(8,128)(2,1)S(1)}, bf16[448,512]{1,0:T(8,128)(2,1)}, u32[]{:S(2)}) copy-start(bf16[448,512]{1,0:T(8,128)(2,1)} %copy-done.6) | copy-start | bytes 1376260
  79.6 12.5 %collective-permute-start.5 = (bf16[4,2,256,256]{3,2,1,0:T(8,128)(2,1)}, bf16[4,2,256,256]{3,2,1,0:T(8,128)(2,1)S(1)}, u32[]{:S(2)}, u32[]{:S(2)}) collective-permute-start(bf16[4,2,256,256]{3,2,1,0:T(8,128)(2,1)} %get-tuple-element.8), channel_id=1, source_target_pairs={{0,32},{32,0},{1,33},{33,1},{2,34},{34,2},{3,35},{35,3},{4,36},{36... | collective-permute-start | bytes 3145736 | tf_op jit(solution)/shard_map/ppermute | solution.py:27
  90.7 3.9 %copy-start.2 = (bf16[512,448]{0,1:T(8,128)(2,1)S(1)}, bf16[512,448]{0,1:T(8,128)(2,1)}, u32[]{:S(2)}) copy-start(bf16[512,448]{0,1:T(8,128)(2,1)} %param.4) | copy-start | bytes 1376260
  92.1 1.0 copy-start.9
  94.6 1.6 %copy-start.5 = (bf16[512,448]{0,1:T(8,128)(2,1)S(1)}, bf16[512,448]{0,1:T(8,128)(2,1)}, u32[]{:S(2)}) copy-start(bf16[512,448]{0,1:T(8,128)(2,1)} %param.5) | copy-start | bytes 1376260
  96.2 4.9 %copy-start.8 = (bf16[448,512]{1,0:T(8,128)(2,1)S(1)}, bf16[448,512]{1,0:T(8,128)(2,1)}, u32[]{:S(2)}) copy-start(bf16[448,512]{1,0:T(8,128)(2,1)} %copy-done.6) | copy-start | bytes 1376260
  99.2 7.3 %collective-permute-start.6 = (f32[256,448]{0,1:T(8,128)S(1)}, f32[256,448]{0,1:T(8,128)S(1)}, u32[]{:S(2)}, u32[]{:S(2)}) collective-permute-start(f32[256,448]{0,1:T(8,128)S(1)} %convolution_add_fusion.6), channel_id=1, source_target_pairs={{0,32},{32,0},{1,33},{33,1},{2,34},{34,2},{3,35},{35,3},{4,36},{36... | collective-permute-start | bytes 1376264 | tf_op jit(solution)/shard_map/ppermute | solution.py:39
  104.0 4.4 %collective-permute-start.11 = (f32[256,448]{0,1:T(8,128)S(1)}, f32[256,448]{0,1:T(8,128)S(1)}, u32[]{:S(2)}, u32[]{:S(2)}) collective-permute-start(f32[256,448]{0,1:T(8,128)S(1)} %convolution_add_fusion), channel_id=1, source_target_pairs={{0,32},{32,0},{1,33},{33,1},{2,34},{34,2},{3,35},{35,3},{4,36},{36... | collective-permute-start | bytes 1376264 | tf_op jit(solution)/shard_map/ppermute | solution.py:39
  110.5 27.8 %collective-permute-start.12 = (f16[128,448]{0,1:T(8,128)(2,1)S(1)}, f16[128,448]{0,1:T(8,128)(2,1)S(1)}, u32[]{:S(2)}, u32[]{:S(2)}) collective-permute-start(f16[128,448]{0,1:T(8,128)(2,1)S(1)} %fusion.39), channel_id=1, source_target_pairs={{0,256},{256,0},{1,257},{257,1},{2,258},{258,2},{3,259},{259,3},{4... | collective-permute-start | bytes 344072 | tf_op jit(solution)/shard_map/ppermute | solution.py:46
  120.9 19.8 %collective-permute-start.7 = (f16[128,448]{0,1:T(8,128)(2,1)S(1)}, f16[128,448]{0,1:T(8,128)(2,1)S(1)}, u32[]{:S(2)}, u32[]{:S(2)}) collective-permute-start(f16[128,448]{0,1:T(8,128)(2,1)S(1)} %fusion.38), channel_id=1, source_target_pairs={{0,256},{256,0},{1,257},{257,1},{2,258},{258,2},{3,259},{259,3},{4... | collective-permute-start | bytes 344072 | tf_op jit(solution)/shard_map/ppermute | solution.py:46

commit v3 on v2

v3 whole, which is shorter than its diff:
```python
import jax
import jax.numpy as jnp
from jax import lax
from jax.sharding import Mesh, PartitionSpec as P

F32 = jnp.float32
AXES = ("h", "i", "q", "zh", "x", "y")
SIZES = (2, 4, 2, 2, 4, 4)
SWAP = [(0, 1), (1, 0)]
RING = [(j, (j + 1) % 4) for j in range(4)]


def body(tokens, gate_weight, up_weight):
    h, i, q, zh = (lax.axis_index(a) for a in ("h", "i", "q", "zh"))
    units = [[gate_weight.T], [up_weight.T]]
    for _ in range(3):
        for k in range(2):
            units[k].append(lax.ppermute(units[k][-1], "i", RING))

    edge = lax.ppermute(tokens, ("h", "zh"), [(2, 0), (1, 3)])
    mid = lax.ppermute(tokens, ("h", "zh"), [(2, 1), (1, 2)])
    far = lax.ppermute(tokens, ("h", "zh"), [(0, 1), (3, 2)])
    away = jnp.where(h == zh, edge, mid)
    keep = jnp.where(h == zh, tokens, far)

    def gather(t):
        whole = lax.all_to_all(jnp.broadcast_to(t[None], (16, 128, 256)), ("x", "y"), 0, 0, tiled=True)
        whole = whole.reshape(4, 2, 2, 128, 256)
        theirs = lax.ppermute(lax.dynamic_index_in_dim(whole, 1 - q, 1, False), "q", SWAP)
        mine = lax.dynamic_index_in_dim(whole, q, 1, False)
        wide = [jnp.concatenate([t[:, 0], t[:, 1]], -1) for t in (theirs, mine)]
        return jnp.concatenate(wide, 1)

    away, keep = gather(away), gather(keep)
    last = {}
    for name, n in (("a", 1), ("k", 5)):
        last[name] = (i + n) & 3

    def product(name, t, k):
        total = 0
        for u in range(4):
            at = last[name] if u == 3 else (i - u) & 3
            rows = lax.dynamic_index_in_dim(t, at, 0, False)
            total = total + lax.dot_general(rows, units[k][u], (((1,), (1,)), ((), ())), preferred_element_type=F32)
        return total[128:] + lax.ppermute(total[:128], "q", SWAP)

    come = []
    for k in range(2):
        part = product("a", away, k)
        if k:
            part, _ = lax.optimization_barrier((part, go))
        go = (16 * part).astype(jnp.float16)
        come.append(lax.ppermute(go, "h", SWAP))
    gate, up = (product("k", keep, k) + come[k].astype(F32) / 16 for k in range(2))
    return (jax.nn.silu(gate) * up).astype(jnp.bfloat16)


def solution(mesh):
    fine = Mesh(mesh.devices.reshape(SIZES), AXES)
    spec = P(("h", "i", "q"), ("zh", "x", "y"))
    return jax.shard_map(body, mesh=fine, in_specs=(spec,) * 3, out_specs=spec, check_vma=False)
```

time: 142 us -> 147 us (1.035)
  waiting for transfers between devices: 45.3 us -> 65.7 us
  starting transfers between devices: 72.1 us -> 59 us
  local copies, waits for them, and re-layouts: 7.07 us -> 4.09 us
    ppermute x7 -> x11, waiting for transfers between devices: 21.7 us -> 39 us  [the longest x1 20.9 us: body(): edge = lax.ppermute(tokens, ('h', 'zh'), [(2, 0), (1, 3)])]
    ppermute x7 -> x11, starting transfers between devices: 42.4 us -> 30.3 us  [the longest x4 9.74 us: product(): return total[128:] + lax.ppermute(total[:128], 'q', SWAP)]
    ppermute x6, starting transfers between devices: 22.8 us -> 16.9 us  [body(): units[k].append(lax.ppermute(units[k][-1], 'i', RING))]
    all_to_all x1 -> x2, starting transfers between devices: 6.89 us -> 11.9 us  [gather(): lax.all_to_all(jnp.broadcast_to(t[None], (16, 128, 256)), ('x', 'y'), 0,...]
    all_to_all x1 -> x2, waiting for transfers between devices: 0.01 us -> 3.47 us  [gather(): lax.all_to_all(jnp.broadcast_to(t[None], (16, 128, 256)), ('x', 'y'), 0,...]
    transpose x3 -> x0, local copies, waits for them, and re-layouts: 3.18 us -> none  [body(): t.transpose(0, 2, 1, 3).reshape(4, 256, 512)]
  transfers between devices with their start and end apart: 14 -> 19, of which waited for: 7 -> 8; matrix products, arithmetic and copies ran while one was open for 13% -> 12% of each run, Pallas kernels for 0% -> 0%
where the time goes in v3:
time: 147 us; the launch traced here: 146 us
  waiting for transfers between devices  65.7 us (45%)
  starting transfers between devices  59 us (40%)
  matrix products  15.2 us (10%)
  local copies, waits for them, and re-layouts  4.09 us (3%)
    ppermute x6, waiting for transfers between devices, body(): units[k].append(lax.ppermute(units[k][-1], 'i', RING))  23.2 us
    ppermute x1, waiting for transfers between devices, body(): edge = lax.ppermute(tokens, ('h', 'zh'), [(2, 0), (1, 3)])  20.9 us
    ppermute x2, waiting for transfers between devices, body(): come.append(lax.ppermute(go, 'h', SWAP))  18 us
    ppermute x6, starting transfers between devices, body(): units[k].append(lax.ppermute(units[k][-1], 'i', RING))  16.9 us
    dot_general x16, matrix products, product(): lax.dot_general(rows, units[k][u], (((1,), (1,)), ((), ())), preferred_el...  15.2 us
    all_to_all x2, starting transfers between devices, gather(): lax.all_to_all(jnp.broadcast_to(t[None], (16, 128, 256)), ('x', 'y'), 0,...  11.9 us
    ppermute x4, starting transfers between devices, product(): return total[128:] + lax.ppermute(total[:128], 'q', SWAP)  9.74 us
    ppermute x2, starting transfers between devices, body(): come.append(lax.ppermute(go, 'h', SWAP))  9.19 us
  transfers between devices with their start and end apart: 19, of which 8 were waited for; matrix products, arithmetic and copies ran while one was open for 12% of the time, Pallas kernels for 0%

profile of v3, /device:TPU:1, one launch (start us, length us, event | category | flops | bytes accessed | tf_op | source)
XLA Modules:
  0.0 145.7 jit_solution(13587270679947637314)
XLA Ops:
  2.0 20.9 %collective-permute-done.6 = bf16[128,256]{1,0:T(8,128)(2,1)S(1)} collective-permute-done((bf16[128,256]{1,0:T(8,128)(2,1)}, bf16[128,256]{1,0:T(8,128)(2,1)S(1)}, u32[]{:S(2)}, u32[]{:S(2)}) %collective-permute-start.6) | collective-permute-done | bytes 65568 | tf_op jit(solution)/shard_map/ppermute | solution.py:20
  24.0 6.9 %all-to-all-start.1 = ((bf16[16,128,256]{2,1,0:T(8,128)(2,1)}), bf16[16,128,256]{2,1,0:T(8,128)(2,1)S(1)}, u32[]{:S(2)}, u32[]{:S(2)}) async-start(bf16[16,128,256]{2,1,0:T(8,128)(2,1)} %broadcast_in_dim.5), calls=%async_computation.1 | async-start | bytes 2097152 | tf_op jit(solution)/shard_map/all_to_all | solution.py:27
  30.9 2.8 %collective-permute-start = (bf16[128,256]{1,0:T(8,128)(2,1)S(1)}, bf16[128,256]{1,0:T(8,128)(2,1)S(1)}, u32[]{:S(2)}, u32[]{:S(2)}) collective-permute-start(bf16[128,256]{1,0:T(8,128)(2,1)S(1)} %copy-done.4), channel_id=1, source_target_pairs={{0,16},{272,256},{1,17},{273,257},{2,18},{274,258},{3,19},{275,259... | collective-permute-start | bytes 196616 | tf_op jit(solution)/shard_map/ppermute | solution.py:22
  33.7 4.3 %collective-permute-start.11 = (bf16[448,512]{1,0:T(8,128)(2,1)S(1)}, bf16[448,512]{1,0:T(8,128)(2,1)}, u32[]{:S(2)}, u32[]{:S(2)}) collective-permute-start(bf16[448,512]{1,0:T(8,128)(2,1)S(1)} %bitcast.98), channel_id=1, source_target_pairs={{0,64},{64,128},{128,192},{192,0},{1,65},{65,129},{129,193},{193,1... | collective-permute-start | bytes 1376264 | tf_op jit(solution)/shard_map/ppermute | solution.py:18
  38.0 4.0 %collective-permute-start.2 = (bf16[448,512]{1,0:T(8,128)(2,1)S(1)}, bf16[448,512]{1,0:T(8,128)(2,1)S(1)}, u32[]{:S(2)}, u32[]{:S(2)}) collective-permute-start(bf16[448,512]{1,0:T(8,128)(2,1)S(1)} %bitcast.99), channel_id=1, source_target_pairs={{0,64},{64,128},{128,192},{192,0},{1,65},{65,129},{129,193},{193,1... | collective-permute-start | bytes 1376264 | tf_op jit(solution)/shard_map/ppermute | solution.py:18
  42.1 3.5 %all-to-all-done.1 = bf16[16,128,256]{2,1,0:T(8,128)(2,1)S(1)} async-done(((bf16[16,128,256]{2,1,0:T(8,128)(2,1)}), bf16[16,128,256]{2,1,0:T(8,128)(2,1)S(1)}, u32[]{:S(2)}, u32[]{:S(2)}) %all-to-all-start.1) | async-done | bytes 1048608 | tf_op jit(solution)/shard_map/all_to_all | solution.py:27
  46.6 5.0 %all-to-all-start = ((bf16[16,128,256]{2,1,0:T(8,128)(2,1)}), bf16[16,128,256]{2,1,0:T(8,128)(2,1)S(1)}, u32[]{:S(2)}, u32[]{:S(2)}) async-start(bf16[16,128,256]{2,1,0:T(8,128)(2,1)} %broadcast_in_dim.4), calls=%async_computation | async-start | bytes 2097152 | tf_op jit(solution)/shard_map/all_to_all | solution.py:27
  52.0 2.8 %collective-permute-start.12 = (bf16[448,512]{1,0:T(8,128)(2,1)}, bf16[448,512]{1,0:T(8,128)(2,1)}, u32[]{:S(2)}, u32[]{:S(2)}) collective-permute-start(bf16[448,512]{1,0:T(8,128)(2,1)} %collective-permute-done.11), channel_id=1, source_target_pairs={{0,64},{64,128},{128,192},{192,0},{1,65},{65,129},{129,193},{193,1... | collective-permute-start | bytes 1376264 | tf_op jit(solution)/shard_map/ppermute | solution.py:18
  54.8 6.9 %collective-permute-done.2 = bf16[448,512]{1,0:T(8,128)(2,1)S(1)} collective-permute-done((bf16[448,512]{1,0:T(8,128)(2,1)S(1)}, bf16[448,512]{1,0:T(8,128)(2,1)S(1)}, u32[]{:S(2)}, u32[]{:S(2)}) %collective-permute-start.2) | collective-permute-done | bytes 458784 | tf_op jit(solution)/shard_map/ppermute | solution.py:18
  61.7 1.9 %collective-permute-start.3 = (bf16[448,512]{1,0:T(8,128)(2,1)S(1)}, bf16[448,512]{1,0:T(8,128)(2,1)}, u32[]{:S(2)}, u32[]{:S(2)}) collective-permute-start(bf16[448,512]{1,0:T(8,128)(2,1)S(1)} %collective-permute-done.2), channel_id=1, source_target_pairs={{0,64},{64,128},{128,192},{192,0},{1,65},{65,129},{129,193},{193,1... | collective-permute-start | bytes 1376264 | tf_op jit(solution)/shard_map/ppermute | solution.py:18
  63.7 8.0 %collective-permute-done.12 = bf16[448,512]{1,0:T(8,128)(2,1)} collective-permute-done((bf16[448,512]{1,0:T(8,128)(2,1)}, bf16[448,512]{1,0:T(8,128)(2,1)}, u32[]{:S(2)}, u32[]{:S(2)}) %collective-permute-start.12) | collective-permute-done | bytes 458784 | tf_op jit(solution)/shard_map/ppermute | solution.py:18
  71.7 1.9 %collective-permute-start.13 = (bf16[448,512]{1,0:T(8,128)(2,1)}, bf16[448,512]{1,0:T(8,128)(2,1)}, u32[]{:S(2)}, u32[]{:S(2)}) collective-permute-start(bf16[448,512]{1,0:T(8,128)(2,1)} %collective-permute-done.12), channel_id=1, source_target_pairs={{0,64},{64,128},{128,192},{192,0},{1,65},{65,129},{129,193},{193,1... | collective-permute-start | bytes 1376264 | tf_op jit(solution)/shard_map/ppermute | solution.py:18
  73.6 7.9 %collective-permute-done.3 = bf16[448,512]{1,0:T(8,128)(2,1)} collective-permute-done((bf16[448,512]{1,0:T(8,128)(2,1)S(1)}, bf16[448,512]{1,0:T(8,128)(2,1)}, u32[]{:S(2)}, u32[]{:S(2)}) %collective-permute-start.3) | collective-permute-done | bytes 458784 | tf_op jit(solution)/shard_map/ppermute | solution.py:18
  81.5 1.9 %collective-permute-start.4 = (bf16[448,512]{1,0:T(8,128)(2,1)}, bf16[448,512]{1,0:T(8,128)(2,1)}, u32[]{:S(2)}, u32[]{:S(2)}) collective-permute-start(bf16[448,512]{1,0:T(8,128)(2,1)} %collective-permute-done.3), channel_id=1, source_target_pairs={{0,64},{64,128},{128,192},{192,0},{1,65},{65,129},{129,193},{193,1... | collective-permute-start | bytes 1376264 | tf_op jit(solution)/shard_map/ppermute | solution.py:18
  84.3 4.8 %collective-permute-start.8 = (bf16[4,2,128,256]{3,2,1,0:T(8,128)(2,1)}, bf16[4,2,128,256]{3,2,1,0:T(8,128)(2,1)S(1)}, u32[]{:S(2)}, u32[]{:S(2)}) collective-permute-start(bf16[4,2,128,256]{3,2,1,0:T(8,128)(2,1)} %get-tuple-element.7), channel_id=1, source_target_pairs={{0,32},{32,0},{1,33},{33,1},{2,34},{34,2},{3,35},{35,3},{4,36},{36... | collective-permute-start | bytes 1572872 | tf_op jit(solution)/shard_map/ppermute | solution.py:29
  89.2 1.9 %collective-permute-start.1 = (bf16[4,2,128,256]{3,2,1,0:T(8,128)(2,1)S(1)}, bf16[4,2,128,256]{3,2,1,0:T(8,128)(2,1)S(1)}, u32[]{:S(2)}, u32[]{:S(2)}) collective-permute-start(bf16[4,2,128,256]{3,2,1,0:T(8,128)(2,1)S(1)} %get-tuple-element.9), channel_id=1, source_target_pairs={{0,32},{32,0},{1,33},{33,1},{2,34},{34,2},{3,35},{35,3},{4,36},{36... | collective-permute-start | bytes 1572872 | tf_op jit(solution)/shard_map/ppermute | solution.py:29
  95.8 2.4 %collective-permute-start.15 = (f32[128,448]{0,1:T(8,128)S(1)}, f32[128,448]{0,1:T(8,128)S(1)}, u32[]{:S(2)}, u32[]{:S(2)}) collective-permute-start(f32[128,448]{0,1:T(8,128)S(1)} %slice.79), channel_id=1, source_target_pairs={{0,32},{32,0},{1,33},{33,1},{2,34},{34,2},{3,35},{35,3},{4,36},{36... | collective-permute-start | bytes 688136 | tf_op jit(solution)/shard_map/ppermute | solution.py:45
  103.1 3.0 %collective-permute-start.9 = (f32[128,448]{0,1:T(8,128)S(1)}, f32[128,448]{0,1:T(8,128)S(1)}, u32[]{:S(2)}, u32[]{:S(2)}) collective-permute-start(f32[128,448]{0,1:T(8,128)S(1)} %slice.75), channel_id=1, source_target_pairs={{0,32},{32,0},{1,33},{33,1},{2,34},{34,2},{3,35},{35,3},{4,36},{36... | collective-permute-start | bytes 688136 | tf_op jit(solution)/shard_map/ppermute | solution.py:45
  110.1 1.9 %collective-permute-start.14 = (f32[128,448]{0,1:T(8,128)S(1)}, f32[128,448]{0,1:T(8,128)S(1)}, u32[]{:S(2)}, u32[]{:S(2)}) collective-permute-start(f32[128,448]{0,1:T(8,128)S(1)} %slice.77), channel_id=1, source_target_pairs={{0,32},{32,0},{1,33},{33,1},{2,34},{34,2},{3,35},{35,3},{4,36},{36... | collective-permute-start | bytes 688136 | tf_op jit(solution)/shard_map/ppermute | solution.py:45
  115.1 2.4 %collective-permute-start.5 = (f32[128,448]{0,1:T(8,128)S(1)}, f32[128,448]{0,1:T(8,128)S(1)}, u32[]{:S(2)}, u32[]{:S(2)}) collective-permute-start(f32[128,448]{0,1:T(8,128)S(1)} %slice.69), channel_id=1, source_target_pairs={{0,32},{32,0},{1,33},{33,1},{2,34},{34,2},{3,35},{35,3},{4,36},{36... | collective-permute-start | bytes 688136 | tf_op jit(solution)/shard_map/ppermute | solution.py:45
  117.6 1.9 %collective-permute-start.16 = (f16[128,448]{0,1:T(8,128)(2,1)S(1)}, f16[128,448]{0,1:T(8,128)(2,1)S(1)}, u32[]{:S(2)}, u32[]{:S(2)}) collective-permute-start(f16[128,448]{0,1:T(8,128)(2,1)S(1)} %multiply_convert_fusion), channel_id=1, source_target_pairs={{0,256},{256,0},{1,257},{257,1},{2,258},{258,2},{3,259},{259,3},{4... | collective-permute-start | bytes 344072 | tf_op jit(solution)/shard_map/ppermute | solution.py:53
  119.6 7.3 %collective-permute-start.10 = (f16[128,448]{0,1:T(8,128)(2,1)S(1)}, f16[128,448]{0,1:T(8,128)(2,1)S(1)}, u32[]{:S(2)}, u32[]{:S(2)}) collective-permute-start(f16[128,448]{0,1:T(8,128)(2,1)S(1)} %fusion.40), channel_id=1, source_target_pairs={{0,256},{256,0},{1,257},{257,1},{2,258},{258,2},{3,259},{259,3},{4... | collective-permute-start | bytes 344072 | tf_op jit(solution)/shard_map/ppermute | solution.py:53
  126.9 15.6 %collective-permute-done.16 = f16[128,448]{0,1:T(8,128)(2,1)S(1)} collective-permute-done((f16[128,448]{0,1:T(8,128)(2,1)S(1)}, f16[128,448]{0,1:T(8,128)(2,1)S(1)}, u32[]{:S(2)}, u32[]{:S(2)}) %collective-permute-start.16) | collective-permute-done | bytes 114720 | tf_op jit(solution)/shard_map/ppermute | solution.py:53
  142.5 2.5 %collective-permute-done.10 = f16[128,448]{0,1:T(8,128)(2,1)S(1)} collective-permute-done((f16[128,448]{0,1:T(8,128)(2,1)S(1)}, f16[128,448]{0,1:T(8,128)(2,1)S(1)}, u32[]{:S(2)}, u32[]{:S(2)}) %collective-permute-start.10) | collective-permute-done | bytes 114720 | tf_op jit(solution)/shard_map/ppermute | solution.py:53
  (60 shorter events, 22.8 us)
Async XLA Ops:
  0.0 2.0 %collective-permute-start.7 = (bf16[128,256]{1,0:T(8,128)(2,1)}, bf16[128,256]{1,0:T(8,128)(2,1)S(1)}, u32[]{:S(2)}, u32[]{:S(2)}) collective-permute-start(bf16[128,256]{1,0:T(8,128)(2,1)} %param.3), channel_id=1, source_target_pairs={{256,16},{16,256},{257,17},{17,257},{258,18},{18,258},{259,19},{19... | collective-permute-start | bytes 196616 | tf_op jit(solution)/shard_map/ppermute | solution.py:21
  0.7 22.3 %collective-permute-start.6 = (bf16[128,256]{1,0:T(8,128)(2,1)}, bf16[128,256]{1,0:T(8,128)(2,1)S(1)}, u32[]{:S(2)}, u32[]{:S(2)}) collective-permute-start(bf16[128,256]{1,0:T(8,128)(2,1)} %param.3), channel_id=1, source_target_pairs={{256,0},{16,272},{257,1},{17,273},{258,2},{18,274},{259,3},{19,275... | collective-permute-start | bytes 196616 | tf_op jit(solution)/shard_map/ppermute | solution.py:20
  24.0 6.9 %copy-start.4 = (bf16[128,256]{1,0:T(8,128)(2,1)S(1)}, bf16[128,256]{1,0:T(8,128)(2,1)}, u32[]{:S(2)}) copy-start(bf16[128,256]{1,0:T(8,128)(2,1)} %param.3) | copy-start | bytes 196612
  24.0 9.7 %copy-start = (bf16[512,448]{0,1:T(8,128)(2,1)S(1)}, bf16[512,448]{0,1:T(8,128)(2,1)}, u32[]{:S(2)}) copy-start(bf16[512,448]{0,1:T(8,128)(2,1)} %param.5) | copy-start | bytes 1376260
  24.0 14.0 %copy-start.1 = (bf16[512,448]{0,1:T(8,128)(2,1)S(1)}, bf16[512,448]{0,1:T(8,128)(2,1)}, u32[]{:S(2)}) copy-start(bf16[512,448]{0,1:T(8,128)(2,1)} %param.4) | copy-start | bytes 1376260
  24.0 21.5 %all-to-all-start.1 = ((bf16[16,128,256]{2,1,0:T(8,128)(2,1)}), bf16[16,128,256]{2,1,0:T(8,128)(2,1)S(1)}, u32[]{:S(2)}, u32[]{:S(2)}) async-start(bf16[16,128,256]{2,1,0:T(8,128)(2,1)} %broadcast_in_dim.5), calls=%async_computation.1 | async-start | bytes 2097152 | tf_op jit(solution)/shard_map/all_to_all | solution.py:27
  30.9 11.1 %collective-permute-start = (bf16[128,256]{1,0:T(8,128)(2,1)S(1)}, bf16[128,256]{1,0:T(8,128)(2,1)S(1)}, u32[]{:S(2)}, u32[]{:S(2)}) collective-permute-start(bf16[128,256]{1,0:T(8,128)(2,1)S(1)} %copy-done.4), channel_id=1, source_target_pairs={{0,16},{272,256},{1,17},{273,257},{2,18},{274,258},{3,19},{275,259... | collective-permute-start | bytes 196616 | tf_op jit(solution)/shard_map/ppermute | solution.py:22
  33.7 18.3 %collective-permute-start.11 = (bf16[448,512]{1,0:T(8,128)(2,1)S(1)}, bf16[448,512]{1,0:T(8,128)(2,1)}, u32[]{:S(2)}, u32[]{:S(2)}) collective-permute-start(bf16[448,512]{1,0:T(8,128)(2,1)S(1)} %bitcast.98), channel_id=1, source_target_pairs={{0,64},{64,128},{128,192},{192,0},{1,65},{65,129},{129,193},{193,1... | collective-permute-start | bytes 1376264 | tf_op jit(solution)/shard_map/ppermute | solution.py:18
  38.0 23.7 %collective-permute-start.2 = (bf16[448,512]{1,0:T(8,128)(2,1)S(1)}, bf16[448,512]{1,0:T(8,128)(2,1)S(1)}, u32[]{:S(2)}, u32[]{:S(2)}) collective-permute-start(bf16[448,512]{1,0:T(8,128)(2,1)S(1)} %bitcast.99), channel_id=1, source_target_pairs={{0,64},{64,128},{128,192},{192,0},{1,65},{65,129},{129,193},{193,1... | collective-permute-start | bytes 1376264 | tf_op jit(solution)/shard_map/ppermute | solution.py:18
  46.6 42.5 %all-to-all-start = ((bf16[16,128,256]{2,1,0:T(8,128)(2,1)}), bf16[16,128,256]{2,1,0:T(8,128)(2,1)S(1)}, u32[]{:S(2)}, u32[]{:S(2)}) async-start(bf16[16,128,256]{2,1,0:T(8,128)(2,1)} %broadcast_in_dim.4), calls=%async_computation | async-start | bytes 2097152 | tf_op jit(solution)/shard_map/all_to_all | solution.py:27
  52.0 19.7 %collective-permute-start.12 = (bf16[448,512]{1,0:T(8,128)(2,1)}, bf16[448,512]{1,0:T(8,128)(2,1)}, u32[]{:S(2)}, u32[]{:S(2)}) collective-permute-start(bf16[448,512]{1,0:T(8,128)(2,1)} %collective-permute-done.11), channel_id=1, source_target_pairs={{0,64},{64,128},{128,192},{192,0},{1,65},{65,129},{129,193},{193,1... | collective-permute-start | bytes 1376264 | tf_op jit(solution)/shard_map/ppermute | solution.py:18
  61.7 21.7 %copy-start.2 = (bf16[448,512]{1,0:T(8,128)(2,1)}, bf16[448,512]{1,0:T(8,128)(2,1)S(1)}, u32[]{:S(2)}) copy-start(bf16[448,512]{1,0:T(8,128)(2,1)S(1)} %collective-permute-done.2) | copy-start | bytes 1376260
  61.7 19.8 %collective-permute-start.3 = (bf16[448,512]{1,0:T(8,128)(2,1)S(1)}, bf16[448,512]{1,0:T(8,128)(2,1)}, u32[]{:S(2)}, u32[]{:S(2)}) collective-permute-start(bf16[448,512]{1,0:T(8,128)(2,1)S(1)} %collective-permute-done.2), channel_id=1, source_target_pairs={{0,64},{64,128},{128,192},{192,0},{1,65},{65,129},{129,193},{193,1... | collective-permute-start | bytes 1376264 | tf_op jit(solution)/shard_map/ppermute | solution.py:18
  71.7 22.7 %collective-permute-start.13 = (bf16[448,512]{1,0:T(8,128)(2,1)}, bf16[448,512]{1,0:T(8,128)(2,1)}, u32[]{:S(2)}, u32[]{:S(2)}) collective-permute-start(bf16[448,512]{1,0:T(8,128)(2,1)} %collective-permute-done.12), channel_id=1, source_target_pairs={{0,64},{64,128},{128,192},{192,0},{1,65},{65,129},{129,193},{193,1... | collective-permute-start | bytes 1376264 | tf_op jit(solution)/shard_map/ppermute | solution.py:18
  81.5 20.2 %collective-permute-start.4 = (bf16[448,512]{1,0:T(8,128)(2,1)}, bf16[448,512]{1,0:T(8,128)(2,1)}, u32[]{:S(2)}, u32[]{:S(2)}) collective-permute-start(bf16[448,512]{1,0:T(8,128)(2,1)} %collective-permute-done.3), channel_id=1, source_target_pairs={{0,64},{64,128},{128,192},{192,0},{1,65},{65,129},{129,193},{193,1... | collective-permute-start | bytes 1376264 | tf_op jit(solution)/shard_map/ppermute | solution.py:18
  84.3 6.9 %collective-permute-start.8 = (bf16[4,2,128,256]{3,2,1,0:T(8,128)(2,1)}, bf16[4,2,128,256]{3,2,1,0:T(8,128)(2,1)S(1)}, u32[]{:S(2)}, u32[]{:S(2)}) collective-permute-start(bf16[4,2,128,256]{3,2,1,0:T(8,128)(2,1)} %get-tuple-element.7), channel_id=1, source_target_pairs={{0,32},{32,0},{1,33},{33,1},{2,34},{34,2},{3,35},{35,3},{4,36},{36... | collective-permute-start | bytes 1572872 | tf_op jit(solution)/shard_map/ppermute | solution.py:29
  89.2 9.3 %collective-permute-start.1 = (bf16[4,2,128,256]{3,2,1,0:T(8,128)(2,1)S(1)}, bf16[4,2,128,256]{3,2,1,0:T(8,128)(2,1)S(1)}, u32[]{:S(2)}, u32[]{:S(2)}) collective-permute-start(bf16[4,2,128,256]{3,2,1,0:T(8,128)(2,1)S(1)} %get-tuple-element.9), channel_id=1, source_target_pairs={{0,32},{32,0},{1,33},{33,1},{2,34},{34,2},{3,35},{35,3},{4,36},{36... | collective-permute-start | bytes 1572872 | tf_op jit(solution)/shard_map/ppermute | solution.py:29
  95.8 21.7 %collective-permute-start.15 = (f32[128,448]{0,1:T(8,128)S(1)}, f32[128,448]{0,1:T(8,128)S(1)}, u32[]{:S(2)}, u32[]{:S(2)}) collective-permute-start(f32[128,448]{0,1:T(8,128)S(1)} %slice.79), channel_id=1, source_target_pairs={{0,32},{32,0},{1,33},{33,1},{2,34},{34,2},{3,35},{35,3},{4,36},{36... | collective-permute-start | bytes 688136 | tf_op jit(solution)/shard_map/ppermute | solution.py:45
  98.7 1.0 copy-start.3
  103.1 14.5 %collective-permute-start.9 = (f32[128,448]{0,1:T(8,128)S(1)}, f32[128,448]{0,1:T(8,128)S(1)}, u32[]{:S(2)}, u32[]{:S(2)}) collective-permute-start(f32[128,448]{0,1:T(8,128)S(1)} %slice.75), channel_id=1, source_target_pairs={{0,32},{32,0},{1,33},{33,1},{2,34},{34,2},{3,35},{35,3},{4,36},{36... | collective-permute-start | bytes 688136 | tf_op jit(solution)/shard_map/ppermute | solution.py:45
  110.1 16.7 %collective-permute-start.14 = (f32[128,448]{0,1:T(8,128)S(1)}, f32[128,448]{0,1:T(8,128)S(1)}, u32[]{:S(2)}, u32[]{:S(2)}) collective-permute-start(f32[128,448]{0,1:T(8,128)S(1)} %slice.77), channel_id=1, source_target_pairs={{0,32},{32,0},{1,33},{33,1},{2,34},{34,2},{3,35},{35,3},{4,36},{36... | collective-permute-start | bytes 688136 | tf_op jit(solution)/shard_map/ppermute | solution.py:45
  115.1 11.8 %collective-permute-start.5 = (f32[128,448]{0,1:T(8,128)S(1)}, f32[128,448]{0,1:T(8,128)S(1)}, u32[]{:S(2)}, u32[]{:S(2)}) collective-permute-start(f32[128,448]{0,1:T(8,128)S(1)} %slice.69), channel_id=1, source_target_pairs={{0,32},{32,0},{1,33},{33,1},{2,34},{34,2},{3,35},{35,3},{4,36},{36... | collective-permute-start | bytes 688136 | tf_op jit(solution)/shard_map/ppermute | solution.py:45
  117.6 24.8 %collective-permute-start.16 = (f16[128,448]{0,1:T(8,128)(2,1)S(1)}, f16[128,448]{0,1:T(8,128)(2,1)S(1)}, u32[]{:S(2)}, u32[]{:S(2)}) collective-permute-start(f16[128,448]{0,1:T(8,128)(2,1)S(1)} %multiply_convert_fusion), channel_id=1, source_target_pairs={{0,256},{256,0},{1,257},{257,1},{2,258},{258,2},{3,259},{259,3},{4... | collective-permute-start | bytes 344072 | tf_op jit(solution)/shard_map/ppermute | solution.py:53
  119.6 25.3 %collective-permute-start.10 = (f16[128,448]{0,1:T(8,128)(2,1)S(1)}, f16[128,448]{0,1:T(8,128)(2,1)S(1)}, u32[]{:S(2)}, u32[]{:S(2)}) collective-permute-start(f16[128,448]{0,1:T(8,128)(2,1)S(1)} %fusion.40), channel_id=1, source_target_pairs={{0,256},{256,0},{1,257},{257,1},{2,258},{258,2},{3,259},{259,3},{4... | collective-permute-start | bytes 344072 | tf_op jit(solution)/shard_map/ppermute | solution.py:53
